TPU v7x, 32 devices: a whole 2x2x4 slice. The times are simulated.
32 devices in a mesh: fsdp: 4 (over z), ctx: 4 (over x, core), tp: 2 (over y).
Axes of the slice: x: 2, y: 2, z: 4, core: 2. Of those that a mesh axis runs over, the one named last changes fastest.
Arguments:
- tokens: bfloat16 [4, 1536, 2048], P('fsdp', 'ctx'), may hold values from -6 to 6
- seq_ids: int32 [4, 1536], P('fsdp'), may hold values from 0 to 2, never falling along the last dimension, each value on 1 to 768 neighbouring positions
- pic_starts: int32 [4, 3], P('fsdp'), may hold values from 0 to 1408, as said below
- pic_lengths: int32 [4, 3], P('fsdp'), may hold values from 128 to 256, as said below
- skip_mask: int32 [4, 1536], P('fsdp', 'ctx'), may hold values 0 or 1
- w_query: bfloat16 [2048, 2048], P('fsdp', 'tp'), may hold values from -0.125 to 0.125
- w_key: bfloat16 [2048, 512], P('fsdp', 'tp'), may hold values from -0.125 to 0.125
- w_value: bfloat16 [2048, 512], P('fsdp', 'tp'), may hold values from -0.125 to 0.125
- w_out: bfloat16 [2048, 2048], P('tp', 'fsdp'), may hold values from -1 to 1
- w_gate: bfloat16 [2048, 5632], P('fsdp', 'tp'), may hold values from -0.125 to 0.125
- w_up: bfloat16 [2048, 5632], P('fsdp', 'tp'), may hold values from -0.125 to 0.125
- w_down: bfloat16 [5632, 2048], P('tp', 'fsdp'), may hold values from -0.078125 to 0.078125
- gain_attn: bfloat16 [2048], P('fsdp'), may hold values from 0.25 to 1.75
- gain_ffn: bfloat16 [2048], P('fsdp'), may hold values from 0.25 to 1.75
- cotangent: bfloat16 [4, 1536, 2048], P('fsdp', 'ctx'), may hold values from -6 to 6
Outputs:
- output: bfloat16 [4, 1536, 2048], P('fsdp', 'ctx')
- input_grad: bfloat16 [4, 1536, 2048], P('fsdp', 'ctx')
- grad_query: float32 [2048, 2048], P('fsdp', 'tp')
- grad_key: float32 [2048, 512], P('fsdp', 'tp')
- grad_value: float32 [2048, 512], P('fsdp', 'tp')
- grad_out: float32 [2048, 2048], P('tp', 'fsdp')
- grad_gate: float32 [2048, 5632], P('fsdp', 'tp')
- grad_up: float32 [2048, 5632], P('fsdp', 'tp')
- grad_down: float32 [5632, 2048], P('tp', 'fsdp')
- grad_gain_attn: float32 [2048], P('fsdp')
- grad_gain_ffn: float32 [2048], P('fsdp')
Inputs may be any that keep to these rules, and one draw needn't show every extreme that they name: `pic_starts`: picture p of a row (counting from 0) lies inside positions p * 2 * 256 to (p + 1) * 2 * 256 - 1, so pictures never intersect; it may start anywhere in that range where it fits. `pic_lengths`: every row has a picture of exactly 256 positions and another of exactly 128.
All inputs are finite; a program needn't handle non-finite values. No bound on the sum of `skip_mask` on one device may be relied on, other than what follows from the above.
Results may differ from a plain program's by a relative error of at most 0.022.
Values may be sent and summed in bfloat16 or wider, within the bound.
No kernel may reach another device: no remote copies, remote signals or barrier semaphores. Data moves between devices by JAX's collectives and lax.ppermute only.
A program may use at most 256 MiB of HBM per device.

v0:
```python
import math
import jax
import jax.numpy as jnp
from jax import lax
from jax.sharding import PartitionSpec as P

HEAD = 128
norm_eps = 1e-05
rope_base = 10000.0


def rotate(values_in, positions, sign):
    half_width = values_in.shape[-1] // 2
    frequency = jnp.power(
        rope_base, -jnp.arange(half_width, dtype=jnp.float32) * 2.0 / values_in.shape[-1]
    )
    angles = positions.astype(jnp.float32)[:, None] * frequency[None, :]
    cosine = jnp.cos(angles)[:, None, :]
    sine_val = sign * jnp.sin(angles)[:, None, :]
    first_half = values_in[..., :half_width]
    second = values_in[..., half_width:]
    return jnp.concatenate(
        [first_half * cosine - second * sine_val, second * cosine + first_half * sine_val], axis=-1
    )


def picture_ids(starts, lengths, positions):
    inside = (positions[:, None] >= starts[None, :]) & (
        positions[:, None] < starts[None, :] + lengths[None, :]
    )
    numbers = jnp.arange(1, starts.shape[0] + 1, dtype=jnp.int32)
    return jnp.sum(jnp.where(inside, numbers[None, :], 0), axis=1)


def allowed_mask(query_pos, key_pos, query_doc, key_doc, query_pic, key_pic):
    same_doc = query_doc[:, None] == key_doc[None, :]
    causal = key_pos[None, :] <= query_pos[:, None]
    picture = (query_pic[:, None] == key_pic[None, :]) & (query_pic[:, None] > 0)
    return same_doc & (causal | picture)


def norm_back(d_normed, hat, inv_rms, gain):
    scaled = d_normed * gain
    return inv_rms * (scaled - hat * jnp.mean(scaled * hat, axis=-1, keepdims=True))


def body(
    tokens,
    seq_ids,
    pic_starts,
    pic_lengths,
    skip_mask,
    w_query,
    w_key,
    w_value,
    w_out,
    w_gate,
    w_up,
    w_down,
    gain_attn,
    gain_ffn,
    cotangent,
):
    tok_rows = tokens.shape[1]
    seq_len = seq_ids.shape[1]
    local_q = w_query.shape[1] // HEAD
    local_kv = w_key.shape[1] // HEAD
    group_size = local_q // local_kv
    query_scale = 1.0 / math.sqrt(HEAD)
    offset = lax.axis_index("ctx") * tok_rows
    positions = offset + jnp.arange(tok_rows, dtype=jnp.int32)
    all_pos = jnp.arange(seq_len, dtype=jnp.int32)
    pic_all = picture_ids(pic_starts[0], pic_lengths[0], all_pos)
    doc_all = seq_ids[0]
    query_doc = lax.dynamic_slice_in_dim(doc_all, offset, tok_rows)
    query_pic = lax.dynamic_slice_in_dim(pic_all, offset, tok_rows)
    allowed = allowed_mask(positions, all_pos, query_doc, doc_all, query_pic, pic_all)

    def attn_weights():
        return (
            lax.all_gather(w_query, "fsdp", axis=0, tiled=True),
            lax.all_gather(w_key, "fsdp", axis=0, tiled=True),
            lax.all_gather(w_value, "fsdp", axis=0, tiled=True),
            lax.all_gather(w_out, "fsdp", axis=1, tiled=True),
            lax.all_gather(gain_attn, "fsdp", axis=0, tiled=True),
        )

    def ffn_weights():
        return (
            lax.all_gather(w_gate, "fsdp", axis=0, tiled=True),
            lax.all_gather(w_up, "fsdp", axis=0, tiled=True),
            lax.all_gather(w_down, "fsdp", axis=1, tiled=True),
            lax.all_gather(gain_ffn, "fsdp", axis=0, tiled=True),
        )

    inputs_f = tokens[0].astype(jnp.float32)
    full_query, full_key, full_value, full_out, gain_one = attn_weights()
    inv_one = lax.rsqrt(jnp.mean(inputs_f * inputs_f, axis=-1, keepdims=True) + norm_eps)
    hat_one = inputs_f * inv_one
    normed_one = (hat_one * gain_one.astype(jnp.float32)).astype(jnp.bfloat16)
    query_pre = jnp.dot(normed_one, full_query, preferred_element_type=jnp.float32)
    key_pre = jnp.dot(normed_one, full_key, preferred_element_type=jnp.float32)
    value_pre = jnp.dot(normed_one, full_value, preferred_element_type=jnp.float32)
    queries = (
        rotate(query_pre.reshape(tok_rows, local_q, HEAD), positions, 1.0) * query_scale
    ).astype(jnp.bfloat16)
    keys_local = rotate(key_pre.reshape(tok_rows, local_kv, HEAD), positions, 1.0).astype(
        jnp.bfloat16
    )
    values_local = value_pre.astype(jnp.bfloat16)
    keys_all, values_all = (
        lax.all_gather(keys_local.reshape(tok_rows, local_kv * HEAD), "ctx", axis=0, tiled=True),
        lax.all_gather(values_local, "ctx", axis=0, tiled=True),
    )
    query_groups = queries.reshape(tok_rows, local_kv, group_size, HEAD)
    key_heads = keys_all.reshape(seq_len, local_kv, HEAD)
    value_heads = values_all.reshape(seq_len, local_kv, HEAD)
    head_outs = []
    log_totals = []
    for kv_index in range(local_kv):
        scores = jnp.einsum(
            "qgd,kd->gqk",
            query_groups[:, kv_index],
            key_heads[:, kv_index],
            preferred_element_type=jnp.float32,
        )
        masked = jnp.where(allowed[None], scores, -1e30)
        row_max = jnp.max(masked, axis=-1, keepdims=True)
        exp_scores = jnp.exp(masked - row_max)
        row_total = jnp.sum(exp_scores, axis=-1, keepdims=True)
        soft_b = (exp_scores / row_total).astype(jnp.bfloat16)
        head_outs.append(
            jnp.einsum(
                "gqk,kd->qgd", soft_b, value_heads[:, kv_index], preferred_element_type=jnp.float32
            )
        )
        log_totals.append(row_max + jnp.log(row_total))
    head_out = jnp.stack(head_outs, axis=1).reshape(tok_rows, local_q * HEAD).astype(jnp.bfloat16)
    attn = lax.psum(jnp.dot(head_out, full_out, preferred_element_type=jnp.float32), "tp")
    keep_f = skip_mask[0].astype(jnp.float32)[:, None]
    mid = inputs_f + keep_f * attn
    full_gate, full_up, full_down, gain_two = ffn_weights()
    inv_two = lax.rsqrt(jnp.mean(mid * mid, axis=-1, keepdims=True) + norm_eps)
    hat_two = mid * inv_two
    normed_two = (hat_two * gain_two.astype(jnp.float32)).astype(jnp.bfloat16)
    gate_act = jnp.dot(normed_two, full_gate, preferred_element_type=jnp.float32)
    up_act = jnp.dot(normed_two, full_up, preferred_element_type=jnp.float32)
    hidden_b = (jax.nn.silu(gate_act) * up_act).astype(jnp.bfloat16)
    ffn = lax.psum(
        jnp.dot(hidden_b, full_down, preferred_element_type=jnp.float32).astype(jnp.bfloat16), "tp"
    ).astype(jnp.float32)
    output = (mid + keep_f * ffn).astype(jnp.bfloat16)
    full_gate, full_up, full_down, gain_two = ffn_weights()
    d_out_f = cotangent[0].astype(jnp.float32)
    d_ffn = (keep_f * d_out_f).astype(jnp.bfloat16)
    grad_down = jnp.einsum("tf,td->fd", hidden_b, d_ffn, preferred_element_type=jnp.float32)
    d_hidden = jnp.einsum("td,fd->tf", d_ffn, full_down, preferred_element_type=jnp.float32)
    sigmoid_gate = jax.nn.sigmoid(gate_act)
    d_up = (d_hidden * (gate_act * sigmoid_gate)).astype(jnp.bfloat16)
    d_gate = (d_hidden * up_act * sigmoid_gate * (1.0 + gate_act * (1.0 - sigmoid_gate))).astype(
        jnp.bfloat16
    )
    grad_gate = jnp.einsum("td,tf->df", normed_two, d_gate, preferred_element_type=jnp.float32)
    grad_up = jnp.einsum("td,tf->df", normed_two, d_up, preferred_element_type=jnp.float32)
    d_norm_part = jnp.einsum(
        "tf,df->td", d_gate, full_gate, preferred_element_type=jnp.float32
    ) + jnp.einsum("tf,df->td", d_up, full_up, preferred_element_type=jnp.float32)
    d_norm_two = lax.psum(d_norm_part, "tp")
    grad_gain_two = jnp.sum(d_norm_two * hat_two, axis=0)
    d_mid = d_out_f + norm_back(d_norm_two, hat_two, inv_two, gain_two.astype(jnp.float32))
    full_query, full_key, full_value, full_out, gain_one = attn_weights()
    d_attn = (keep_f * d_mid).astype(jnp.bfloat16)
    grad_out = jnp.einsum("tc,td->cd", head_out, d_attn, preferred_element_type=jnp.float32)
    d_head = jnp.einsum("td,cd->tc", d_attn, full_out, preferred_element_type=jnp.float32).astype(
        jnp.bfloat16
    )
    d_head_groups = d_head.reshape(tok_rows, local_kv, group_size, HEAD)
    d_query_list = []
    d_key_list = []
    d_value_list = []
    for kv_index in range(local_kv):
        scores = jnp.einsum(
            "qgd,kd->gqk",
            query_groups[:, kv_index],
            key_heads[:, kv_index],
            preferred_element_type=jnp.float32,
        )
        soft_f = jnp.where(allowed[None], jnp.exp(scores - log_totals[kv_index]), 0.0)
        soft_b = soft_f.astype(jnp.bfloat16)
        d_soft = jnp.einsum(
            "qgd,kd->gqk",
            d_head_groups[:, kv_index],
            value_heads[:, kv_index],
            preferred_element_type=jnp.float32,
        )
        row_delta = jnp.sum(soft_f * d_soft, axis=-1, keepdims=True)
        d_scores = (soft_f * (d_soft - row_delta)).astype(jnp.bfloat16)
        d_query_list.append(
            jnp.einsum(
                "gqk,kd->qgd", d_scores, key_heads[:, kv_index], preferred_element_type=jnp.float32
            )
        )
        d_key_list.append(
            jnp.einsum(
                "gqk,qgd->kd",
                d_scores,
                query_groups[:, kv_index],
                preferred_element_type=jnp.float32,
            )
        )
        d_value_list.append(
            jnp.einsum(
                "gqk,qgd->kd",
                soft_b,
                d_head_groups[:, kv_index],
                preferred_element_type=jnp.float32,
            )
        )
    d_keys_all = jnp.stack(d_key_list, axis=1).reshape(seq_len, local_kv * HEAD)
    d_values_all = jnp.stack(d_value_list, axis=1).reshape(seq_len, local_kv * HEAD)
    d_keys, d_values = (
        lax.psum_scatter(
            d_keys_all.astype(jnp.bfloat16), "ctx", scatter_dimension=0, tiled=True
        ).astype(jnp.float32),
        lax.psum_scatter(
            d_values_all.astype(jnp.bfloat16), "ctx", scatter_dimension=0, tiled=True
        ).astype(jnp.float32),
    )
    d_queries = jnp.stack(d_query_list, axis=1).reshape(tok_rows, local_q, HEAD)
    d_query_pre = (
        (rotate(d_queries, positions, -1.0) * query_scale)
        .reshape(tok_rows, local_q * HEAD)
        .astype(jnp.bfloat16)
    )
    d_key_pre = (
        rotate(d_keys.reshape(tok_rows, local_kv, HEAD), positions, -1.0)
        .reshape(tok_rows, local_kv * HEAD)
        .astype(jnp.bfloat16)
    )
    d_value_pre = d_values.astype(jnp.bfloat16)
    grad_query = jnp.einsum(
        "td,tc->dc", normed_one, d_query_pre, preferred_element_type=jnp.float32
    )
    grad_key = jnp.einsum("td,tc->dc", normed_one, d_key_pre, preferred_element_type=jnp.float32)
    grad_value = jnp.einsum(
        "td,tc->dc", normed_one, d_value_pre, preferred_element_type=jnp.float32
    )
    d_norm_part_one = (
        jnp.einsum("tc,dc->td", d_query_pre, full_query, preferred_element_type=jnp.float32)
        + jnp.einsum("tc,dc->td", d_key_pre, full_key, preferred_element_type=jnp.float32)
        + jnp.einsum("tc,dc->td", d_value_pre, full_value, preferred_element_type=jnp.float32)
    )
    d_norm_one = lax.psum(d_norm_part_one.astype(jnp.bfloat16), "tp").astype(jnp.float32)
    grad_gain_one = jnp.sum(d_norm_one * hat_one, axis=0)
    input_grad = (
        d_mid + norm_back(d_norm_one, hat_one, inv_one, gain_one.astype(jnp.float32))
    ).astype(jnp.bfloat16)
    (
        shard_query,
        shard_key,
        shard_value,
        shard_out,
        shard_gain_one,
        shard_gate,
        shard_up,
        shard_down,
        shard_gain_two,
    ) = (
        lax.psum_scatter(
            grad_query.astype(jnp.bfloat16), "fsdp", scatter_dimension=0, tiled=True
        ).astype(jnp.float32),
        lax.psum_scatter(
            grad_key.astype(jnp.bfloat16), "fsdp", scatter_dimension=0, tiled=True
        ).astype(jnp.float32),
        lax.psum_scatter(
            grad_value.astype(jnp.bfloat16), "fsdp", scatter_dimension=0, tiled=True
        ).astype(jnp.float32),
        lax.psum_scatter(
            grad_out.astype(jnp.bfloat16), "fsdp", scatter_dimension=1, tiled=True
        ).astype(jnp.float32),
        lax.psum_scatter(
            grad_gain_one.astype(jnp.bfloat16), "fsdp", scatter_dimension=0, tiled=True
        ).astype(jnp.float32),
        lax.psum_scatter(
            grad_gate.astype(jnp.bfloat16), "fsdp", scatter_dimension=0, tiled=True
        ).astype(jnp.float32),
        lax.psum_scatter(
            grad_up.astype(jnp.bfloat16), "fsdp", scatter_dimension=0, tiled=True
        ).astype(jnp.float32),
        lax.psum_scatter(
            grad_down.astype(jnp.bfloat16), "fsdp", scatter_dimension=1, tiled=True
        ).astype(jnp.float32),
        lax.psum_scatter(
            grad_gain_two.astype(jnp.bfloat16), "fsdp", scatter_dimension=0, tiled=True
        ).astype(jnp.float32),
    )
    summed = (
        lax.psum(shard_query.astype(jnp.bfloat16), "ctx").astype(jnp.float32),
        lax.psum(shard_key.astype(jnp.bfloat16), "ctx").astype(jnp.float32),
        lax.psum(shard_value.astype(jnp.bfloat16), "ctx").astype(jnp.float32),
        lax.psum(shard_out.astype(jnp.bfloat16), "ctx").astype(jnp.float32),
        lax.psum(shard_gate.astype(jnp.bfloat16), "ctx").astype(jnp.float32),
        lax.psum(shard_up.astype(jnp.bfloat16), "ctx").astype(jnp.float32),
        lax.psum(shard_down.astype(jnp.bfloat16), "ctx").astype(jnp.float32),
        lax.psum(shard_gain_one.astype(jnp.bfloat16), "ctx").astype(jnp.float32),
        lax.psum(shard_gain_two.astype(jnp.bfloat16), "ctx").astype(jnp.float32),
    )
    return (
        output[None],
        input_grad[None],
        summed[0],
        summed[1],
        summed[2],
        summed[3],
        summed[4],
        summed[5],
        summed[6],
        summed[7],
        summed[8],
    )


def solution(mesh):
    placed = (
        P("fsdp", "ctx", None),
        P("fsdp", None),
        P("fsdp", None),
        P("fsdp", None),
        P("fsdp", "ctx"),
        P("fsdp", "tp"),
        P("fsdp", "tp"),
        P("fsdp", "tp"),
        P("tp", "fsdp"),
        P("fsdp", "tp"),
        P("fsdp", "tp"),
        P("tp", "fsdp"),
        P("fsdp"),
        P("fsdp"),
        P("fsdp", "ctx", None),
    )
    return jax.shard_map(
        body,
        mesh=mesh,
        in_specs=placed,
        out_specs=(
            P("fsdp", "ctx", None),
            P("fsdp", "ctx", None),
            P("fsdp", "tp"),
            P("fsdp", "tp"),
            P("fsdp", "tp"),
            P("tp", "fsdp"),
            P("fsdp", "tp"),
            P("fsdp", "tp"),
            P("tp", "fsdp"),
            P("fsdp"),
            P("fsdp"),
        ),
        check_vma=False,
    )
```

profile of v0, /device:TPU:0, one launch (start us, length us, event | category | flops | bytes accessed | tf_op | source)
XLA Modules:
  0.0 2267.5 jit_solution(3418881602823138451)
XLA Ops:
  12.6 13.7 all-gather
  28.8 11.5 all-gather.10.cloned.1.call-done
  51.9 17.4 all-gather.12.cloned.1.call-done
  73.7 9.0 all_gather.46
  82.7 68.4 %all-gather.14.cloned.1.call-done = bf16[2048,1024]{1,0:T(8,128)(2,1)} async-done(((bf16[512,1024]{1,0:T(8,128)(2,1)}), bf16[2048,1024]{1,0:T(8,128)(2,1)}) %all-gather.14.cloned.1.call-update) | async-done | bytes 4194320 | tf_op jit(solution)/shard_map/all_gather | solution.py:81
  181.2 50.7 %all-gather.16.cloned.1.call-done = bf16[1024,2048]{1,0:T(8,128)(2,1)} async-done(((bf16[1024,512]{1,0:T(8,128)(2,1)}), bf16[1024,2048]{1,0:T(8,128)(2,1)}) %all-gather.16.cloned.1.call-update) | async-done | bytes 4194320 | tf_op jit(solution)/shard_map/all_gather | solution.py:84
  239.8 11.9 all-gather.1
  251.8 70.4 %all-reduce.11.cloned.1.call-done = f32[384,2048]{1,0:T(8,128)} async-done(((f32[384,2048]{1,0:T(8,128)}), f32[384,2048]{1,0:T(8,128)}) %all-reduce.11.cloned.1.call-update) | async-done | bytes 3145744 | tf_op jit(solution)/shard_map/psum | solution.py:139
  326.6 198.1 %all-gather.20.cloned.1.call-done = bf16[2048,2816]{1,0:T(8,128)(2,1)} async-done(((bf16[512,2816]{1,0:T(8,128)(2,1)}), bf16[2048,2816]{1,0:T(8,128)(2,1)}) %all-gather.20.cloned.1.call-update) | async-done | bytes 11534352 | tf_op jit(solution)/shard_map/all_gather | solution.py:91
  524.7 11.4 fusion.104
  536.2 189.5 %all-gather.18.cloned.1.call-done = bf16[2048,2816]{1,0:T(8,128)(2,1)} async-done(((bf16[512,2816]{1,0:T(8,128)(2,1)}), bf16[2048,2816]{1,0:T(8,128)(2,1)}) %all-gather.18.cloned.1.call-update) | async-done | bytes 11534352 | tf_op jit(solution)/shard_map/all_gather | solution.py:90
  725.6 11.4 fusion.103
  737.1 189.5 %all-gather.22.cloned.1.call-done = bf16[2816,2048]{1,0:T(8,128)(2,1)} async-done(((bf16[2816,512]{1,0:T(8,128)(2,1)}), bf16[2816,2048]{1,0:T(8,128)(2,1)}) %all-gather.22.cloned.1.call-update) | async-done | bytes 11534352 | tf_op jit(solution)/shard_map/all_gather | solution.py:92
  926.6 12.9 multiply_convert_fusion
  939.5 9.1 fusion.105
  948.6 10.6 convolution_add_fusion
  959.3 84.0 %all-reduce.13.cloned.1.call-done = f32[384,2048]{1,0:T(8,128)} async-done(((f32[384,2048]{1,0:T(8,128)}), f32[384,2048]{1,0:T(8,128)}) %all-reduce.13.cloned.1.call-update) | async-done | bytes 3145744 | tf_op jit(solution)/shard_map/psum | solution.py:168
  1074.0 16.4 fusion.3
  1090.4 13.9 fusion.5
  1116.6 20.1 reduce-scatter.28.cloned.1.call-done
  1161.1 11.0 convolution_convert_fusion.2
  1172.2 10.7 convolution_convert_fusion
  1183.2 10.8 convolution_convert_fusion.1
  1194.0 10.9 convolution_convert_fusion.5
  1210.1 63.4 %reduce-scatter.20.cloned.1.call-done = bf16[1024,512]{1,0:T(8,128)(2,1)} async-done(((bf16[1024,2048]{1,0:T(8,128)(2,1)}), bf16[1024,512]{1,0:T(8,128)(2,1)}) %reduce-scatter.20.cloned.1.call-update) | async-done | bytes 1048592 | tf_op jit(solution)/shard_map/reduce_scatter | solution.py:278
  1273.5 80.1 %reduce-scatter.14.cloned.1.call-done = bf16[512,1024]{1,0:T(8,128)(2,1)} async-done(((bf16[2048,1024]{1,0:T(8,128)(2,1)}), bf16[512,1024]{1,0:T(8,128)(2,1)}) %reduce-scatter.14.cloned.1.call-update) | async-done | bytes 1048592 | tf_op jit(solution)/shard_map/reduce_scatter | solution.py:269
  1353.6 197.7 %reduce-scatter.26.cloned.1.call-done = bf16[2816,512]{1,0:T(8,128)(2,1)} async-done(((bf16[2816,2048]{1,0:T(8,128)(2,1)}), bf16[2816,512]{1,0:T(8,128)(2,1)}) %reduce-scatter.26.cloned.1.call-update) | async-done | bytes 2883600 | tf_op jit(solution)/shard_map/reduce_scatter | solution.py:290
  1551.3 198.2 %reduce-scatter.24.cloned.1.call-done = bf16[512,2816]{1,0:T(8,128)(2,1)} async-done(((bf16[2048,2816]{1,0:T(8,128)(2,1)}), bf16[512,2816]{1,0:T(8,128)(2,1)}) %reduce-scatter.24.cloned.1.call-update) | async-done | bytes 2883600 | tf_op jit(solution)/shard_map/reduce_scatter | solution.py:287
  1749.5 198.2 %reduce-scatter.22.cloned.1.call-done = bf16[512,2816]{1,0:T(8,128)(2,1)} async-done(((bf16[2048,2816]{1,0:T(8,128)(2,1)}), bf16[512,2816]{1,0:T(8,128)(2,1)}) %reduce-scatter.22.cloned.1.call-update) | async-done | bytes 2883600 | tf_op jit(solution)/shard_map/reduce_scatter | solution.py:284
  1949.6 88.1 %all-reduce.17.cloned.1.call-done = (bf16[384,2048]{1,0:T(8,128)(2,1)}, bf16[384,2048]{1,0:T(8,128)(2,1)}) async-done(((bf16[384,2048]{1,0:T(8,128)(2,1)}, bf16[384,2048]{1,0:T(8,128)(2,1)}), (bf16[384,2048]{1,0:T(8,128)(2,1)}, bf16[384,2048]{1,0:T(8,128)(2,1)})) %all-reduce.17.cloned.1.call-update) | async-done | bytes 3145744 | tf_op jit(solution)/shard_map/psum | solution.py:149
  2040.7 11.9 all-reduce.4
  2066.4 176.6 %all-reduce.15.cloned.1.call-done = (bf16[512,1024]{1,0:T(8,128)(2,1)}, bf16[512,256]{1,0:T(8,128)(2,1)}, bf16[512,256]{1,0:T(8,128)(2,1)}, bf16[1024,512]{1,0:T...) async-done(((bf16[512,1024]{1,0:T(8,128)(2,1)}, bf16[512,256]{1,0:T(8,128)(2,1)}, bf16[512,256]{1,0:T(8,128)(2,1)}, ...) | async-done | bytes 11272208 | tf_op jit(solution)/shard_map/psum | solution.py:298
  (238 shorter events, 173.7 us)
Async XLA Ops:
  7.2 19.1 copy-start.44
  7.2 19.1 copy-start.45
  7.2 33.1 %all-gather.10.cloned.1.call-start = ((), (), s32[]{:S(2)}) async-start(), calls=%async_computation.9 | async-start | bytes 1310720 | tf_op jit(solution)/shard_map/all_gather | solution.py:83
  7.9 61.4 %all-gather.12.cloned.1.call-start = ((), (), s32[]{:S(2)}) async-start(), calls=%async_computation.10 | async-start | bytes 1310720 | tf_op jit(solution)/shard_map/all_gather | solution.py:82
  8.7 142.5 %all-gather.14.cloned.1.call-start = ((), (), s32[]{:S(2)}) async-start(), calls=%async_computation.11 | async-start | bytes 5242880 | tf_op jit(solution)/shard_map/all_gather | solution.py:81
  9.4 222.5 %all-gather.16.cloned.1.call-start = ((), (), s32[]{:S(2)}) async-start(), calls=%async_computation.12 | async-start | bytes 5242880 | tf_op jit(solution)/shard_map/all_gather | solution.py:84
  10.0 312.1 %all-reduce.11.cloned.1.call-start = ((), (), s32[]{:S(2)}) async-start(), calls=%async_computation.13 | async-start | bytes 6291456 | tf_op jit(solution)/shard_map/psum | solution.py:139
  12.6 145.2 %copy-start.39 = (f32[384]{0:T(512)}, f32[384]{0:T(512)S(1)}, u32[]{:S(2)}) copy-start(f32[384]{0:T(512)S(1)} %add_rsqrt_fusion.1) | copy-start | bytes 4612
  26.3 131.5 %copy-start.35 = (f32[4,1,512]{2,1,0:T(1,128)}, f32[4,1,512]{2,1,0:T(1,128)S(1)}, u32[]{:S(2)}) copy-start(f32[4,1,512]{2,1,0:T(1,128)S(1)} %convert_element_type.301) | copy-start | bytes 24580
  27.6 135.2 %copy-start.26 = (f32[384,64]{0,1:T(8,128)}, f32[384,64]{0,1:T(8,128)S(1)}, u32[]{:S(2)}) copy-start(f32[384,64]{0,1:T(8,128)S(1)} %get-tuple-element.53) | copy-start | bytes 294916
  28.8 149.4 %copy-start.7 = (pred[384,1536]{0,1:T(8,128)(4,1)}, pred[384,1536]{0,1:T(8,128)(4,1)S(1)}, u32[]{:S(2)}) copy-start(pred[384,1536]{0,1:T(8,128)(4,1)S(1)} %fusion.58) | copy-start | bytes 1769476
  181.2 56.4 %copy-start.19 = (bf16[384,2,4,128]{0,3,2,1:T(8,128)(2,1)}, bf16[384,2,4,128]{0,3,2,1:T(8,128)(2,1)S(1)}, u32[]{:S(2)}) copy-start(bf16[384,2,4,128]{0,3,2,1:T(8,128)(2,1)S(1)} %pad_maximum_fusion.1) | copy-start | bytes 2359300
  237.7 287.1 %all-gather.20.cloned.1.call-start = ((), (), s32[]{:S(2)}) async-start(), calls=%async_computation.15 | async-start | bytes 14417920 | tf_op jit(solution)/shard_map/all_gather | solution.py:91
  238.3 487.4 %all-gather.18.cloned.1.call-start = ((), (), s32[]{:S(2)}) async-start(), calls=%async_computation.14 | async-start | bytes 14417920 | tf_op jit(solution)/shard_map/all_gather | solution.py:90
  239.0 687.6 %all-gather.22.cloned.1.call-start = ((), (), s32[]{:S(2)}) async-start(), calls=%async_computation.16 | async-start | bytes 14417920 | tf_op jit(solution)/shard_map/all_gather | solution.py:92
  239.8 803.6 %all-reduce.13.cloned.1.call-start = ((), (), s32[]{:S(2)}) async-start(), calls=%async_computation.17 | async-start | bytes 6291456 | tf_op jit(solution)/shard_map/psum | solution.py:168
  251.7 796.0 %copy-start.37 = (f32[384]{0:T(512)}, f32[384]{0:T(512)S(1)}, u32[]{:S(2)}) copy-start(f32[384]{0:T(512)S(1)} %convert_reduce_fusion) | copy-start | bytes 4612
  959.3 153.9 %reduce-scatter.30.cloned.1.call-start = ((), (), s32[]{:S(2)}) async-start(), calls=%async_computation.26 | async-start | bytes 983040
  1073.9 62.7 %reduce-scatter.28.cloned.1.call-start = ((), (), s32[]{:S(2)}) async-start(), calls=%async_computation.25 | async-start | bytes 983040
  1073.9 16.4 copy-start.9
  1113.1 24.7 %copy-start.27 = (f32[384,64]{0,1:T(8,128)S(1)}, f32[384,64]{0,1:T(8,128)}, u32[]{:S(2)}) copy-start(f32[384,64]{0,1:T(8,128)} %copy-done.26) | copy-start | bytes 294916
  1113.1 24.7 %copy-start.31 = (f32[384,64]{0,1:T(8,128)S(1)}, f32[384,64]{0,1:T(8,128)}, u32[]{:S(2)}) copy-start(f32[384,64]{0,1:T(8,128)} %get-tuple-element.51) | copy-start | bytes 294916
  1113.1 96.9 %reduce-scatter.18.cloned.1.call-start = ((), (), s32[]{:S(2)}) async-start(), calls=%async_computation.20 | async-start | bytes 1310720 | tf_op jit(solution)/shard_map/reduce_scatter | solution.py:275
  1116.5 93.6 %reduce-scatter.16.cloned.1.call-start = ((), (), s32[]{:S(2)}) async-start(), calls=%async_computation.19 | async-start | bytes 1310720 | tf_op jit(solution)/shard_map/reduce_scatter | solution.py:272
  1141.2 132.3 %reduce-scatter.20.cloned.1.call-start = ((), (), s32[]{:S(2)}) async-start(), calls=%async_computation.21 | async-start | bytes 5242880 | tf_op jit(solution)/shard_map/reduce_scatter | solution.py:278
  1147.8 205.8 %reduce-scatter.14.cloned.1.call-start = ((), (), s32[]{:S(2)}) async-start(), calls=%async_computation.18 | async-start | bytes 5242880 | tf_op jit(solution)/shard_map/reduce_scatter | solution.py:269
  1161.0 390.2 %reduce-scatter.26.cloned.1.call-start = ((), (), s32[]{:S(2)}) async-start(), calls=%async_computation.24 | async-start | bytes 14417920 | tf_op jit(solution)/shard_map/reduce_scatter | solution.py:290
  1172.1 577.4 %reduce-scatter.24.cloned.1.call-start = ((), (), s32[]{:S(2)}) async-start(), calls=%async_computation.23 | async-start | bytes 14417920 | tf_op jit(solution)/shard_map/reduce_scatter | solution.py:287
  1182.9 764.8 %reduce-scatter.22.cloned.1.call-start = ((), (), s32[]{:S(2)}) async-start(), calls=%async_computation.22 | async-start | bytes 14417920 | tf_op jit(solution)/shard_map/reduce_scatter | solution.py:284
  1193.9 843.7 %all-reduce.17.cloned.1.call-start = ((), (), s32[]{:S(2)}) async-start(), calls=%async_computation.28 | async-start | bytes 6291456 | tf_op jit(solution)/shard_map/psum | solution.py:149
  1210.0 1033.0 %all-reduce.15.cloned.1.call-start = ((), (), s32[]{:S(2)}) async-start(), calls=%async_computation.27 | async-start | bytes 22544384 | tf_op jit(solution)/shard_map/psum | solution.py:298
  1947.7 92.9 %copy-start.41 = (bf16[2048]{0:T(1024)(128)(2,1)S(1)}, bf16[2048]{0:T(1024)(128)(2,1)}, u32[]{:S(2)}) copy-start(bf16[2048]{0:T(1024)(128)(2,1)} %get-tuple-element.11) | copy-start | bytes 12292
  (40 other events, 192.4 us)
Sparse Core Ops, SparseCore 0:
  9.6 30.6 all-gather.9
  41.9 27.3 all-gather.11
  70.9 80.2 all-gather.13
  152.6 79.2 all-gather.15
  237.8 84.2 all-reduce.10
  323.6 201.0 all-gather.19
  526.4 199.2 all-gather.17
  727.3 199.2 all-gather.21
  959.4 83.9 all-reduce.12
  1074.0 23.2 reduce-scatter.29
  1113.2 23.3 reduce-scatter.27
  1139.3 27.1 reduce-scatter.17
  1169.5 25.7 reduce-scatter.15
  1198.0 75.4 reduce-scatter.19
  1276.3 77.2 reduce-scatter.13
  1355.8 195.4 reduce-scatter.25
  1553.5 195.9 reduce-scatter.23
  1751.7 195.9 reduce-scatter.21
  1950.7 86.9 all-reduce.16
  2041.1 201.7 all-reduce.14
where the time goes:
time: 2270 us
  waiting for transfers between devices  1910 us (84%)
  matrix products  189 us (8%)
  blocking collectives  61.3 us (3%)
  other arithmetic  60.2 us (3%)
  local copies, waits for them, and re-layouts  32.7 us (1%)
    reduce_scatter x1, waiting for transfers between devices, body(): lax.psum_scatter(grad_gate.astype(jnp.bfloat16), 'fsdp', scatter_dimensio...  198 us
    reduce_scatter x1, waiting for transfers between devices, body(): lax.psum_scatter(grad_up.astype(jnp.bfloat16), 'fsdp', scatter_dimension=...  198 us
    all_gather x1, waiting for transfers between devices, ffn_weights(): lax.all_gather(w_up, 'fsdp', axis=0, tiled=True)  198 us
    reduce_scatter x1, waiting for transfers between devices, body(): lax.psum_scatter(grad_down.astype(jnp.bfloat16), 'fsdp', scatter_dimensio...  198 us
    all_gather x1, waiting for transfers between devices, ffn_weights(): lax.all_gather(w_gate, 'fsdp', axis=0, tiled=True)  189 us
    all_gather x1, waiting for transfers between devices, ffn_weights(): lax.all_gather(w_down, 'fsdp', axis=1, tiled=True)  189 us
    psum x1, waiting for transfers between devices, body(): lax.psum(shard_query.astype(jnp.bfloat16), 'ctx').astype(jnp.float32)  177 us
    psum x1, waiting for transfers between devices, body(): lax.psum(jnp.dot(hidden_b, full_down, preferred_element_type=jnp.float32)...  88.1 us
  transfers between devices with their start and end apart: 20, of which 17 were waited for; matrix products, arithmetic and copies ran while one was open for 8% of the time, Pallas kernels for 0%

commit v1 on v0

--- a/solution.py
+++ b/solution.py
@@ -1,12 +1,45 @@
+import functools
 import math
 import jax
 import jax.numpy as jnp
 from jax import lax
 from jax.sharding import PartitionSpec as P
+from jax.lax import axis_index, axis_size, ppermute
 
 HEAD = 128
 norm_eps = 1e-05
 rope_base = 10000.0
+
+
+def compute_pieces_all(packet, d0):
+    packet = jnp.moveaxis(packet, 0, d0)
+    raw_out = packet.shape
+    o_now = packet.reshape(*raw_out[:d0], raw_out[d0] * raw_out[d0 + 1], *raw_out[d0 + 2 :])
+    return o_now
+
+
+def recast_sites(payload, along_axis):
+    shaped, res = (axis_size(along_axis), axis_index(along_axis))
+    newest, carry_out = (payload[None], 1)
+    while carry_out < shaped:
+        nodes = []
+        for c in range(shaped):
+            nodes.append((c, c ^ carry_out))
+        reply = ppermute(newest, along_axis, nodes)
+        work_now = res & carry_out == 0
+        newest = jnp.concatenate(
+            [jnp.where(work_now, newest, reply), jnp.where(work_now, reply, newest)]
+        )
+        carry_out *= 2
+    return newest
+
+
+def pair_blocks(frame, sheet, k_dim):
+    then = compute_pieces_all(recast_sites(frame, sheet), k_dim)
+    return then
+
+
+name_pages = functools.partial(pair_blocks, sheet="fsdp", k_dim=0)
 
 
 def rotate(values_in, positions, sign):
@@ -78,7 +111,7 @@
 
     def attn_weights():
         return (
-            lax.all_gather(w_query, "fsdp", axis=0, tiled=True),
+            name_pages(w_query),
             lax.all_gather(w_key, "fsdp", axis=0, tiled=True),
             lax.all_gather(w_value, "fsdp", axis=0, tiled=True),
             lax.all_gather(w_out, "fsdp", axis=1, tiled=True),

time: 2270 us -> 2310 us (1.018)
  blocking collectives: 61.3 us -> 93.5 us
    ppermute x0 -> x2, waiting for transfers between devices: none -> 84 us  [recast_sites(): reply = ppermute(newest, along_axis, nodes)]
    all_gather x1 -> x0, waiting for transfers between devices: 68.4 us -> none  [attn_weights(): lax.all_gather(w_query, 'fsdp', axis=0, tiled=True)]
    all_gather x1, waiting for transfers between devices: 50.7 us -> 0.02 us  [attn_weights(): lax.all_gather(w_out, 'fsdp', axis=1, tiled=True)]
    all_gather x1, waiting for transfers between devices: 17.4 us -> 53.9 us  [attn_weights(): lax.all_gather(w_key, 'fsdp', axis=0, tiled=True)]
    all_gather x1, blocking collectives: 13.7 us -> 45.7 us  [attn_weights(): lax.all_gather(gain_attn, 'fsdp', axis=0, tiled=True)]
  transfers between devices with their start and end apart: 20 -> 21, of which waited for: 17 -> 15; matrix products, arithmetic and copies ran while one was open for 8% -> 9% of each run, Pallas kernels for 0% -> 0%
where the time goes in v1:
time: 2310 us; the launch traced here: 2300 us
  waiting for transfers between devices  1890 us (82%)
  matrix products  189 us (8%)
  blocking collectives  93.5 us (4%)
  other arithmetic  70.4 us (3%)
  local copies, waits for them, and re-layouts  34.9 us (2%)
    reduce_scatter x1, waiting for transfers between devices, body(): lax.psum_scatter(grad_up.astype(jnp.bfloat16), 'fsdp', scatter_dimension=...  198 us
    reduce_scatter x1, waiting for transfers between devices, body(): lax.psum_scatter(grad_gate.astype(jnp.bfloat16), 'fsdp', scatter_dimensio...  198 us
    all_gather x1, waiting for transfers between devices, ffn_weights(): lax.all_gather(w_up, 'fsdp', axis=0, tiled=True)  198 us
    reduce_scatter x1, waiting for transfers between devices, body(): lax.psum_scatter(grad_down.astype(jnp.bfloat16), 'fsdp', scatter_dimensio...  198 us
    all_gather x1, waiting for transfers between devices, ffn_weights(): lax.all_gather(w_down, 'fsdp', axis=1, tiled=True)  189 us
    all_gather x1, waiting for transfers between devices, ffn_weights(): lax.all_gather(w_gate, 'fsdp', axis=0, tiled=True)  189 us
    psum x1, waiting for transfers between devices, body(): lax.psum(shard_query.astype(jnp.bfloat16), 'ctx').astype(jnp.float32)  177 us
    psum x1, waiting for transfers between devices, body(): lax.psum(jnp.dot(hidden_b, full_down, preferred_element_type=jnp.float32)...  87.9 us
  transfers between devices with their start and end apart: 21, of which 15 were waited for; matrix products, arithmetic and copies ran while one was open for 9% of the time, Pallas kernels for 0%

profile of v1, /device:TPU:0, one launch (start us, length us, event | category | flops | bytes accessed | tf_op | source)
XLA Modules:
  0.0 2301.7 jit_solution(16815099684039483531)
XLA Ops:
  13.3 45.7 %all-gather = bf16[4,1,512]{2,1,0:T(2,128)(2,1)S(1)} all-gather(bf16[1,1,512]{2,1,0:T(2,128)(2,1)S(1)} %reshape.384), channel_id=1, replica_groups=mesh['fsdp'=4,'ctx'=4,'tp'=2] {'fsdp'}, dimensions={0}, use_global_device_ids=true | all-gather | bytes 5120 | tf_op jit(solution)/shard_map/all_gather | solution.py:118
  70.9 8.6 all_gather.40
  80.7 53.9 %all-gather.11.cloned.1.call-done = bf16[2048,256]{1,0:T(8,128)(2,1)} async-done(((bf16[512,256]{1,0:T(8,128)(2,1)}), bf16[2048,256]{1,0:T(8,128)(2,1)}) %all-gather.11.cloned.1.call-update) | async-done | bytes 1048592 | tf_op jit(solution)/shard_map/all_gather | solution.py:115
  139.1 9.0 all_gather.42
  148.2 84.0 %collective-permute-done.1 = bf16[2,512,1024]{2,1,0:T(8,128)(2,1)} collective-permute-done((bf16[2,512,1024]{2,1,0:T(8,128)(2,1)}, bf16[2,512,1024]{2,1,0:T(8,128)(2,1)}, u32[]{:S(2)}, u32[]{:S(2)}) %collective-permute-start.1) | collective-permute-done | bytes 2097184 | tf_op jit(solution)/shard_map/ppermute | solution.py:28
  236.7 6.6 copy.105
  274.3 11.9 all-gather.1
  286.2 71.1 %all-reduce.11.cloned.1.call-done = f32[384,2048]{1,0:T(8,128)} async-done(((f32[384,2048]{1,0:T(8,128)}), f32[384,2048]{1,0:T(8,128)}) %all-reduce.11.cloned.1.call-update) | async-done | bytes 3145744 | tf_op jit(solution)/shard_map/psum | solution.py:172
  361.8 198.1 %all-gather.17.cloned.1.call-done = bf16[2048,2816]{1,0:T(8,128)(2,1)} async-done(((bf16[512,2816]{1,0:T(8,128)(2,1)}), bf16[2048,2816]{1,0:T(8,128)(2,1)}) %all-gather.17.cloned.1.call-update) | async-done | bytes 11534352 | tf_op jit(solution)/shard_map/all_gather | solution.py:124
  559.9 11.4 fusion.104
  571.3 189.4 %all-gather.15.cloned.1.call-done = bf16[2048,2816]{1,0:T(8,128)(2,1)} async-done(((bf16[512,2816]{1,0:T(8,128)(2,1)}), bf16[2048,2816]{1,0:T(8,128)(2,1)}) %all-gather.15.cloned.1.call-update) | async-done | bytes 11534352 | tf_op jit(solution)/shard_map/all_gather | solution.py:123
  760.7 11.4 fusion.103
  772.1 189.5 %all-gather.19.cloned.1.call-done = bf16[2816,2048]{1,0:T(8,128)(2,1)} async-done(((bf16[2816,512]{1,0:T(8,128)(2,1)}), bf16[2816,2048]{1,0:T(8,128)(2,1)}) %all-gather.19.cloned.1.call-update) | async-done | bytes 11534352 | tf_op jit(solution)/shard_map/all_gather | solution.py:125
  961.6 12.9 multiply_convert_fusion
  974.5 9.1 fusion.105
  983.6 10.6 convolution_add_fusion
  994.3 84.1 %all-reduce.13.cloned.1.call-done = f32[384,2048]{1,0:T(8,128)} async-done(((f32[384,2048]{1,0:T(8,128)}), f32[384,2048]{1,0:T(8,128)}) %all-reduce.13.cloned.1.call-update) | async-done | bytes 3145744 | tf_op jit(solution)/shard_map/psum | solution.py:201
  1109.0 16.4 fusion.3
  1125.4 13.9 fusion.5
  1151.6 20.1 reduce-scatter.28.cloned.1.call-done
  1196.1 11.0 convolution_convert_fusion.2
  1207.2 10.7 convolution_convert_fusion
  1218.1 10.8 convolution_convert_fusion.1
  1229.0 10.8 convolution_convert_fusion.5
  1246.4 61.7 %reduce-scatter.20.cloned.1.call-done = bf16[1024,512]{1,0:T(8,128)(2,1)} async-done(((bf16[1024,2048]{1,0:T(8,128)(2,1)}), bf16[1024,512]{1,0:T(8,128)(2,1)}) %reduce-scatter.20.cloned.1.call-update) | async-done | bytes 1048592 | tf_op jit(solution)/shard_map/reduce_scatter | solution.py:311
  1308.1 80.1 %reduce-scatter.14.cloned.1.call-done = bf16[512,1024]{1,0:T(8,128)(2,1)} async-done(((bf16[2048,1024]{1,0:T(8,128)(2,1)}), bf16[512,1024]{1,0:T(8,128)(2,1)}) %reduce-scatter.14.cloned.1.call-update) | async-done | bytes 1048592 | tf_op jit(solution)/shard_map/reduce_scatter | solution.py:302
  1388.2 197.7 %reduce-scatter.26.cloned.1.call-done = bf16[2816,512]{1,0:T(8,128)(2,1)} async-done(((bf16[2816,2048]{1,0:T(8,128)(2,1)}), bf16[2816,512]{1,0:T(8,128)(2,1)}) %reduce-scatter.26.cloned.1.call-update) | async-done | bytes 2883600 | tf_op jit(solution)/shard_map/reduce_scatter | solution.py:323
  1585.9 198.2 %reduce-scatter.24.cloned.1.call-done = bf16[512,2816]{1,0:T(8,128)(2,1)} async-done(((bf16[2048,2816]{1,0:T(8,128)(2,1)}), bf16[512,2816]{1,0:T(8,128)(2,1)}) %reduce-scatter.24.cloned.1.call-update) | async-done | bytes 2883600 | tf_op jit(solution)/shard_map/reduce_scatter | solution.py:320
  1784.1 198.2 %reduce-scatter.22.cloned.1.call-done = bf16[512,2816]{1,0:T(8,128)(2,1)} async-done(((bf16[2048,2816]{1,0:T(8,128)(2,1)}), bf16[512,2816]{1,0:T(8,128)(2,1)}) %reduce-scatter.22.cloned.1.call-update) | async-done | bytes 2883600 | tf_op jit(solution)/shard_map/reduce_scatter | solution.py:317
  1984.2 87.9 %all-reduce.17.cloned.1.call-done = (bf16[384,2048]{1,0:T(8,128)(2,1)}, bf16[384,2048]{1,0:T(8,128)(2,1)}) async-done(((bf16[384,2048]{1,0:T(8,128)(2,1)}, bf16[384,2048]{1,0:T(8,128)(2,1)}), (bf16[384,2048]{1,0:T(8,128)(2,1)}, bf16[384,2048]{1,0:T(8,128)(2,1)})) %all-reduce.17.cloned.1.call-update) | async-done | bytes 3145744 | tf_op jit(solution)/shard_map/psum | solution.py:182
  2075.1 11.9 all-reduce.4
  2100.8 176.7 %all-reduce.15.cloned.1.call-done = (bf16[512,1024]{1,0:T(8,128)(2,1)}, bf16[512,256]{1,0:T(8,128)(2,1)}, bf16[512,256]{1,0:T(8,128)(2,1)}, bf16[1024,512]{1,0:T...) async-done(((bf16[512,1024]{1,0:T(8,128)(2,1)}, bf16[512,256]{1,0:T(8,128)(2,1)}, bf16[512,256]{1,0:T(8,128)(2,1)}, ...) | async-done | bytes 11272208 | tf_op jit(solution)/shard_map/psum | solution.py:331
  (249 shorter events, 172.6 us)
Async XLA Ops:
  7.2 57.0 %copy-start.33 = (bf16[512,1024]{1,0:T(8,128)(2,1)S(1)}, bf16[512,1024]{1,0:T(8,128)(2,1)}, u32[]{:S(2)}) copy-start(bf16[512,1024]{1,0:T(8,128)(2,1)} %param.20) | copy-start | bytes 3145732
  7.2 61.7 %all-gather.9.cloned.1.call-start = ((), (), s32[]{:S(2)}) async-start(), calls=%async_computation.9 | async-start | bytes 1310720 | tf_op jit(solution)/shard_map/all_gather | solution.py:116
  7.9 126.7 %all-gather.11.cloned.1.call-start = ((), (), s32[]{:S(2)}) async-start(), calls=%async_computation.10 | async-start | bytes 1310720 | tf_op jit(solution)/shard_map/all_gather | solution.py:115
  8.7 257.6 %all-gather.13.cloned.1.call-start = ((), (), s32[]{:S(2)}) async-start(), calls=%async_computation.11 | async-start | bytes 5242880 | tf_op jit(solution)/shard_map/all_gather | solution.py:117
  8.7 55.5 %collective-permute-start = (bf16[1,512,1024]{2,1,0:T(8,128)(2,1)}, bf16[1,512,1024]{2,1,0:T(8,128)(2,1)}, u32[]{:S(2)}, u32[]{:S(2)}) collective-permute-start(bf16[1,512,1024]{2,1,0:T(8,128)(2,1)} %bitcast.332), channel_id=1, source_target_pairs={{0,8},{8,0},{16,24},{24,16},{1,9},{9,1},{17,25},{25,17},{2,10},{10... | collective-permute-start | bytes 3145736 | tf_op jit(solution)/shard_map/ppermute | solution.py:28
  11.8 345.5 %all-reduce.11.cloned.1.call-start = ((), (), s32[]{:S(2)}) async-start(), calls=%async_computation.12 | async-start | bytes 6291456 | tf_op jit(solution)/shard_map/psum | solution.py:172
  59.0 184.3 %copy-start.40 = (f32[4,1,512]{2,1,0:T(1,128)}, f32[4,1,512]{2,1,0:T(1,128)S(1)}, u32[]{:S(2)}) copy-start(f32[4,1,512]{2,1,0:T(1,128)S(1)} %convert_element_type.304) | copy-start | bytes 24580
  63.1 180.2 %copy-start.44 = (f32[384]{0:T(512)}, f32[384]{0:T(512)S(1)}, u32[]{:S(2)}) copy-start(f32[384]{0:T(512)S(1)} %add_rsqrt_fusion.1) | copy-start | bytes 4612
  64.2 183.7 %copy-start.30 = (f32[384,64]{0,1:T(8,128)}, f32[384,64]{0,1:T(8,128)S(1)}, u32[]{:S(2)}) copy-start(f32[384,64]{0,1:T(8,128)S(1)} %get-tuple-element.57) | copy-start | bytes 294916
  67.2 165.0 %collective-permute-start.1 = (bf16[2,512,1024]{2,1,0:T(8,128)(2,1)}, bf16[2,512,1024]{2,1,0:T(8,128)(2,1)}, u32[]{:S(2)}, u32[]{:S(2)}) collective-permute-start(bf16[2,512,1024]{2,1,0:T(8,128)(2,1)} %pad_maximum_fusion.1), channel_id=1, source_target_pairs={{0,16},{8,24},{16,0},{24,8},{1,17},{9,25},{17,1},{25,9},{2,18},{10... | collective-permute-start | bytes 6291464 | tf_op jit(solution)/shard_map/ppermute | solution.py:28
  68.8 194.4 %copy-start.7 = (pred[384,1536]{0,1:T(8,128)(4,1)}, pred[384,1536]{0,1:T(8,128)(4,1)S(1)}, u32[]{:S(2)}) copy-start(pred[384,1536]{0,1:T(8,128)(4,1)S(1)} %fusion.58) | copy-start | bytes 1769476
  136.9 95.3 %copy-start.15 = (bf16[1,512,1024]{2,1,0:T(8,128)(2,1)S(1)}, bf16[1,512,1024]{2,1,0:T(8,128)(2,1)}, u32[]{:S(2)}) copy-start(bf16[1,512,1024]{2,1,0:T(8,128)(2,1)} %copy-done.14) | copy-start | bytes 3145732
  136.9 95.3 %copy-start.17 = (bf16[1,512,1024]{2,1,0:T(8,128)(2,1)S(1)}, bf16[1,512,1024]{2,1,0:T(8,128)(2,1)}, u32[]{:S(2)}) copy-start(bf16[1,512,1024]{2,1,0:T(8,128)(2,1)} %copy-done.16) | copy-start | bytes 3145732
  272.3 287.6 %all-gather.17.cloned.1.call-start = ((), (), s32[]{:S(2)}) async-start(), calls=%async_computation.14 | async-start | bytes 14417920 | tf_op jit(solution)/shard_map/all_gather | solution.py:124
  272.9 487.8 %all-gather.15.cloned.1.call-start = ((), (), s32[]{:S(2)}) async-start(), calls=%async_computation.13 | async-start | bytes 14417920 | tf_op jit(solution)/shard_map/all_gather | solution.py:123
  273.5 688.2 %all-gather.19.cloned.1.call-start = ((), (), s32[]{:S(2)}) async-start(), calls=%async_computation.15 | async-start | bytes 14417920 | tf_op jit(solution)/shard_map/all_gather | solution.py:125
  274.2 804.2 %all-reduce.13.cloned.1.call-start = ((), (), s32[]{:S(2)}) async-start(), calls=%async_computation.16 | async-start | bytes 6291456 | tf_op jit(solution)/shard_map/psum | solution.py:201
  286.2 796.5 %copy-start.42 = (f32[384]{0:T(512)}, f32[384]{0:T(512)S(1)}, u32[]{:S(2)}) copy-start(f32[384]{0:T(512)S(1)} %convert_reduce_fusion) | copy-start | bytes 4612
  994.3 153.9 %reduce-scatter.30.cloned.1.call-start = ((), (), s32[]{:S(2)}) async-start(), calls=%async_computation.25 | async-start | bytes 983040
  1108.9 62.7 %reduce-scatter.28.cloned.1.call-start = ((), (), s32[]{:S(2)}) async-start(), calls=%async_computation.24 | async-start | bytes 983040
  1148.1 24.7 %copy-start.31 = (f32[384,64]{0,1:T(8,128)S(1)}, f32[384,64]{0,1:T(8,128)}, u32[]{:S(2)}) copy-start(f32[384,64]{0,1:T(8,128)} %copy-done.30) | copy-start | bytes 294916
  1148.1 24.7 %copy-start.36 = (f32[384,64]{0,1:T(8,128)S(1)}, f32[384,64]{0,1:T(8,128)}, u32[]{:S(2)}) copy-start(f32[384,64]{0,1:T(8,128)} %get-tuple-element.55) | copy-start | bytes 294916
  1148.1 98.3 %reduce-scatter.18.cloned.1.call-start = ((), (), s32[]{:S(2)}) async-start(), calls=%async_computation.19 | async-start | bytes 1310720 | tf_op jit(solution)/shard_map/reduce_scatter | solution.py:308
  1151.5 94.9 %reduce-scatter.16.cloned.1.call-start = ((), (), s32[]{:S(2)}) async-start(), calls=%async_computation.18 | async-start | bytes 1310720 | tf_op jit(solution)/shard_map/reduce_scatter | solution.py:305
  1176.2 131.9 %reduce-scatter.20.cloned.1.call-start = ((), (), s32[]{:S(2)}) async-start(), calls=%async_computation.20 | async-start | bytes 5242880 | tf_op jit(solution)/shard_map/reduce_scatter | solution.py:311
  1182.8 205.4 %reduce-scatter.14.cloned.1.call-start = ((), (), s32[]{:S(2)}) async-start(), calls=%async_computation.17 | async-start | bytes 5242880 | tf_op jit(solution)/shard_map/reduce_scatter | solution.py:302
  1196.0 389.8 %reduce-scatter.26.cloned.1.call-start = ((), (), s32[]{:S(2)}) async-start(), calls=%async_computation.23 | async-start | bytes 14417920 | tf_op jit(solution)/shard_map/reduce_scatter | solution.py:323
  1207.1 577.0 %reduce-scatter.24.cloned.1.call-start = ((), (), s32[]{:S(2)}) async-start(), calls=%async_computation.22 | async-start | bytes 14417920 | tf_op jit(solution)/shard_map/reduce_scatter | solution.py:320
  1217.9 764.4 %reduce-scatter.22.cloned.1.call-start = ((), (), s32[]{:S(2)}) async-start(), calls=%async_computation.21 | async-start | bytes 14417920 | tf_op jit(solution)/shard_map/reduce_scatter | solution.py:317
  1229.0 843.2 %all-reduce.17.cloned.1.call-start = ((), (), s32[]{:S(2)}) async-start(), calls=%async_computation.27 | async-start | bytes 6291456 | tf_op jit(solution)/shard_map/psum | solution.py:182
  1246.3 1031.2 %all-reduce.15.cloned.1.call-start = ((), (), s32[]{:S(2)}) async-start(), calls=%async_computation.26 | async-start | bytes 22544384 | tf_op jit(solution)/shard_map/psum | solution.py:331
  1982.3 92.8 %copy-start.46 = (bf16[2048]{0:T(1024)(128)(2,1)S(1)}, bf16[2048]{0:T(1024)(128)(2,1)}, u32[]{:S(2)}) copy-start(bf16[2048]{0:T(1024)(128)(2,1)} %get-tuple-element.11) | copy-start | bytes 12292
  (44 other events, 217.3 us)
Sparse Core Ops, SparseCore 0:
  9.6 41.8 all-gather.8
  53.0 81.5 all-gather.10
  136.2 104.5 all-gather.12
  272.4 84.8 all-reduce.10
  358.8 201.0 all-gather.16
  561.4 199.2 all-gather.14
  762.3 199.2 all-gather.18
  994.4 83.9 all-reduce.12
  1109.0 23.2 reduce-scatter.29
  1148.2 23.3 reduce-scatter.27
  1174.5 27.1 reduce-scatter.17
  1204.5 25.7 reduce-scatter.15
  1232.6 75.4 reduce-scatter.19
  1310.9 77.2 reduce-scatter.13
  1390.4 195.4 reduce-scatter.25
  1588.1 195.9 reduce-scatter.23
  1786.3 195.9 reduce-scatter.21
  1985.1 86.9 all-reduce.16
  2075.7 201.7 all-reduce.14
